TPU v7x, 32 devices: a whole 2x2x4 slice. The times are simulated.
32 devices in a mesh: dp: 8 (over y, x, core), tensor: 4 (over z).
Axes of the slice: x: 2, y: 2, z: 4, core: 2. Of those that a mesh axis runs over, the one named last changes fastest.
Arguments:
- hidden_in: bfloat16 [16384, 1024], P(('dp', 'tensor')), may hold values from -6 to 6
- out_grad: bfloat16 [16384, 1024], P(('dp', 'tensor')), may hold values from -6 to 6
- attn_weight: bfloat16 [4, 1024, 1024], P(None, 'dp', 'tensor'), may hold values from -2 to 2
- mlp_weight: bfloat16 [3, 1024, 2624], P(None, 'dp', 'tensor'), may hold values from -2 to 2
- norm_gain: bfloat16 [2, 1024], replicated, may hold values from 0.5 to 1.5
- attn_first: float32 [4, 1024, 1024], P(None, 'dp', 'tensor'), may hold values from -60 to 60
- attn_second: float32 [4, 1024, 1024], P(None, 'dp', 'tensor'), may hold values from 100 to 3000
- attn_left: float32 [4, 1024, 512], P(None, 'dp', 'tensor'), may hold values from -2 to 3
- attn_right: float32 [4, 2048, 1024], P(None, 'dp', 'tensor'), may hold values from -2 to 3
- mlp_first: float32 [3, 1024, 2624], P(None, 'dp', 'tensor'), may hold values from -60 to 60
- mlp_second: float32 [3, 1024, 2624], P(None, 'dp', 'tensor'), may hold values from 100 to 3000
- mlp_left: float32 [3, 1024, 512], P(None, 'dp', 'tensor'), may hold values from -2 to 3
- mlp_right: float32 [3, 5248, 2624], P(None, 'dp', 'tensor'), may hold values from -2 to 3
- gain_first: float32 [2, 1024], replicated, may hold values from -60 to 60
- gain_second: float32 [2, 1024], replicated, may hold values from 100 to 3000
- owner_rows: int32 [8], replicated, may hold values from 0 to 7, each once
- segment_ids: int32 [16384], P('dp'), may hold values from 0 to 15, as said below
- positions: int32 [16384], P('dp'), may hold values from 0 to 1023, as said below
- valid: int32 [16384], P('dp'), may hold values from 0 to 1, as said below
- step: int32 [], replicated, may hold values from 1 to 20
- learn_rate: float32 [], replicated, may hold values from 0.03 to 0.08
- beta_first: float32 [], replicated, may hold values from 0.8 to 0.95
- beta_second: float32 [], replicated, may hold values from 0.9 to 0.99
Outputs:
- output: bfloat16 [16384, 1024], P(('dp', 'tensor'))
- input_grad: bfloat16 [16384, 1024], P(('dp', 'tensor'))
- attn_grad: float32 [4, 1024, 1024], P(None, 'dp', 'tensor')
- mlp_grad: float32 [3, 1024, 2624], P(None, 'dp', 'tensor')
- gain_grad: float32 [2, 1024], replicated
- attn_first_new: float32 [4, 1024, 1024], P(None, 'dp', 'tensor')
- attn_second_new: float32 [4, 1024, 1024], P(None, 'dp', 'tensor')
- mlp_first_new: float32 [3, 1024, 2624], P(None, 'dp', 'tensor')
- mlp_second_new: float32 [3, 1024, 2624], P(None, 'dp', 'tensor')
- gain_first_new: float32 [2, 1024], replicated
- gain_second_new: float32 [2, 1024], replicated
- attn_update: float32 [4, 1024, 1024], P(None, 'dp', 'tensor')
- mlp_update: float32 [3, 1024, 2624], P(None, 'dp', 'tensor')
- gain_update: float32 [2, 1024], replicated
- norm_scale: float32 [7, 8, 4], P(None, 'dp', 'tensor')
- root_means: float32 [4], replicated
Inputs may be any that keep to these rules, and one draw needn't show every extreme that they name: `owner_rows`: each index of dp owns a different row block of 128 rows. `segment_ids`: ids restart at 0 with every sequence of 1024 tokens and never fall within it; every document but the last of a sequence has 64 tokens or more. `positions`: 0 at the start of every sequence and wherever segment_ids changes, else one more than the token before. `valid`: within each sequence: 1 on a leading run of at least half of its tokens, 0 after it.
All inputs are finite; a program needn't handle non-finite values.
Results may differ from a plain program's by a relative error of at most 0.014.
Values may be sent and summed in bfloat16 or wider, within the bound.
No kernel may reach another device: no remote copies, remote signals or barrier semaphores. Data moves between devices by JAX's collectives and lax.ppermute only.
A program may use at most 256 MiB of HBM per device.

v0:
```python
import math

import jax
import jax.numpy as jnp
from jax import lax
from jax.sharding import PartitionSpec as P

D = 1024
HEADS = 16
HEAD_DIM = 64
SEQ_LEN = 1024


NORM_EPS = 1e-05
ROPE_BASE = 160000.0
ADAM_EPS = 1e-08
SCALE_EPS = 1e-06
MASKED = -1e30
PRECISE = lax.Precision.HIGHEST


def layer_norm(values, gain_row):
    average = jnp.mean(values, axis=-1, keepdims=True)
    centred = values - average
    spread = jnp.mean(centred * centred, axis=-1, keepdims=True)
    return centred * lax.rsqrt(spread + NORM_EPS) * gain_row


def rope_tables(positions):
    half_dim = HEAD_DIM // 2
    frequency = jnp.exp(
        jnp.arange(half_dim, dtype=jnp.float32) * (-2.0 * math.log(ROPE_BASE) / HEAD_DIM)
    )
    angles = positions.astype(jnp.float32)[:, None] * frequency[None, :]
    return (jnp.cos(angles)[:, None, :], jnp.sin(angles)[:, None, :])


def rotate(values, cos_table, sin_table):
    half_dim = values.shape[-1] // 2
    lower_half = values[..., :half_dim]
    upper_half = values[..., half_dim:]
    return jnp.concatenate(
        [
            lower_half * cos_table - upper_half * sin_table,
            upper_half * cos_table + lower_half * sin_table,
        ],
        axis=-1,
    )


def rotate_back(grads_in, cos_table, sin_table):
    half_dim = grads_in.shape[-1] // 2
    lower_half = grads_in[..., :half_dim]
    upper_half = grads_in[..., half_dim:]
    return jnp.concatenate(
        [
            lower_half * cos_table + upper_half * sin_table,
            upper_half * cos_table - lower_half * sin_table,
        ],
        axis=-1,
    )


def allowed_mask(seg_block, seg_all, keep_all, block_rows):
    location = jnp.arange(seg_all.shape[0])
    return (seg_block[:, None] == seg_all[None, :]) & (
        (keep_all[None, :] > 0) | (block_rows[:, None] == location[None, :])
    )


def block_scores(query_block, key_rows, seg_all, keep_all, first_row, block_size):
    seg_block = lax.dynamic_slice_in_dim(seg_all, first_row, block_size, 0)
    block_rows = first_row + jnp.arange(block_size)
    allowed = allowed_mask(seg_block, seg_all, keep_all, block_rows)
    raw = jnp.einsum("qhe,khe->hqk", query_block, key_rows, preferred_element_type=jnp.float32)
    return jnp.where(allowed[None], raw * (1.0 / math.sqrt(HEAD_DIM)), MASKED)


def sequence_forward(pieces):
    queries, key_rows, value_rows, seg_all, keep_all = pieces
    length = queries.shape[0]
    block_size = min(512, length)
    block_count = length // block_size

    def one_block(block_index):
        first_row = block_index * block_size
        query_block = lax.dynamic_slice_in_dim(queries, first_row, block_size, 0)
        scores = block_scores(query_block, key_rows, seg_all, keep_all, first_row, block_size)
        highest = jnp.max(scores, axis=-1, keepdims=True)
        exponent = jnp.exp(scores - highest)
        summed = jnp.sum(exponent, axis=-1, keepdims=True)
        weights = (exponent / summed).astype(jnp.bfloat16)
        mixture = jnp.einsum(
            "hqk,khe->qhe", weights, value_rows, preferred_element_type=jnp.float32
        )
        return (mixture, (highest + jnp.log(summed))[..., 0])

    mixture, log_sums = lax.map(one_block, jnp.arange(block_count))
    return (mixture.reshape(length, mixture.shape[2], mixture.shape[3]), log_sums)


def sequence_backward(pieces):
    queries, key_rows, value_rows, seg_all, keep_all, log_sums, mix_grad = pieces
    length = queries.shape[0]
    block_size = min(512, length)
    block_count = length // block_size
    factor = 1.0 / math.sqrt(HEAD_DIM)

    def one_block(carried, block_index):
        key_grad, value_grad = carried
        first_row = block_index * block_size
        query_block = lax.dynamic_slice_in_dim(queries, first_row, block_size, 0)
        scores = block_scores(query_block, key_rows, seg_all, keep_all, first_row, block_size)
        probability = jnp.exp(
            scores - lax.dynamic_index_in_dim(log_sums, block_index, 0, keepdims=False)[..., None]
        )
        weights = probability.astype(jnp.bfloat16)
        grad_block = lax.dynamic_slice_in_dim(mix_grad, first_row, block_size, 0)
        prob_grad = jnp.einsum(
            "qhe,khe->hqk", grad_block, value_rows, preferred_element_type=jnp.float32
        )
        score_grad = probability * (
            prob_grad - jnp.sum(probability * prob_grad, axis=-1, keepdims=True)
        )
        raw_grad = (score_grad * factor).astype(jnp.bfloat16)
        query_grad = jnp.einsum(
            "hqk,khe->qhe", raw_grad, key_rows, preferred_element_type=jnp.float32
        )
        key_grad = key_grad + jnp.einsum(
            "hqk,qhe->khe", raw_grad, query_block, preferred_element_type=jnp.float32
        )
        value_grad = value_grad + jnp.einsum(
            "hqk,qhe->khe", weights, grad_block, preferred_element_type=jnp.float32
        )
        return ((key_grad, value_grad), query_grad)

    zero_rows = jnp.zeros(key_rows.shape, jnp.float32)
    (key_grad, value_grad), query_grad = lax.scan(
        one_block, (zero_rows, zero_rows), jnp.arange(block_count)
    )
    return (query_grad.reshape(queries.shape), key_grad, value_grad)


def to_model(stored, inverse, owners):
    kind_count, row_total, col_total = stored.shape
    return jnp.take(
        stored.reshape(kind_count, owners, row_total // owners, col_total), inverse, axis=1
    ).reshape(kind_count, row_total, col_total)


def to_owner(model, owner_rows, owners):
    kind_count, row_total, col_total = model.shape
    return jnp.take(
        model.reshape(kind_count, owners, row_total // owners, col_total), owner_rows, axis=1
    ).reshape(kind_count, row_total, col_total)


def soap_block(grad_block, first, second, left, right, step_size, beta_one, beta_two):
    half_turn = jnp.einsum("kab,kac->kbc", left, grad_block, precision=PRECISE)
    rotated = jnp.einsum("kbc,kce->kbe", half_turn, right, precision=PRECISE)
    first_new = beta_one * first + (1.0 - beta_one) * rotated
    second_new = beta_two * second + (1.0 - beta_two) * rotated * rotated
    direction = first_new / (jnp.sqrt(second_new) + ADAM_EPS)
    back_half = jnp.einsum("kab,kbe->kae", left, direction, precision=PRECISE)
    turned = jnp.einsum("kae,kce->kac", back_half, right, precision=PRECISE)
    factor = jnp.sqrt(jnp.mean(direction * direction, axis=(1, 2))) * lax.rsqrt(
        jnp.mean(turned * turned, axis=(1, 2)) + SCALE_EPS
    )
    update = -step_size * factor[:, None, None] * turned
    return (first_new, second_new, update, factor)


def gelu_gate(gate_vals, up_vals):
    return jax.nn.gelu(gate_vals, approximate=False) * up_vals


def per_device(
    hidden_in,
    out_grad,
    attn_weight,
    mlp_weight,
    norm_gain,
    attn_first,
    attn_second,
    attn_left,
    attn_right,
    mlp_first,
    mlp_second,
    mlp_left,
    mlp_right,
    gain_first,
    gain_second,
    owner_rows,
    segment_ids,
    positions,
    valid,
    step,
    learn_rate,
    beta_first,
    beta_second,
):
    owners = lax.axis_size("dp")
    shards = lax.axis_size("tensor")
    own_rows = hidden_in.shape[0]
    group_rows = segment_ids.shape[0]
    offset = lax.axis_index("tensor") * own_rows
    heads_here = HEADS // shards
    sequences = group_rows // SEQ_LEN
    gain_rows = norm_gain.astype(jnp.float32)
    hidden_f = hidden_in.astype(jnp.float32)
    attn_stored, mlp_stored = (
        lax.all_gather(attn_weight, "dp", axis=1, tiled=True),
        lax.all_gather(mlp_weight, "dp", axis=1, tiled=True),
    )
    slot_ids = jnp.arange(owners, dtype=jnp.int32)
    inverse = jnp.sum(
        slot_ids[:, None] * (owner_rows[:, None] == slot_ids[None, :]).astype(jnp.int32), axis=0
    )
    attn_model = to_model(attn_stored, inverse, owners)
    mlp_model = to_model(mlp_stored, inverse, owners)
    qkv_local = attn_model[:3]
    out_local = attn_model[3]
    gate_up_local = mlp_model[:2]
    down_local = mlp_model[2]
    first_norm = layer_norm(hidden_f, gain_rows[0]).astype(jnp.bfloat16)
    first_all = lax.all_gather(first_norm, "tensor", axis=0, tiled=True)
    projected = jnp.einsum("td,kdc->ktc", first_all, qkv_local, preferred_element_type=jnp.float32)
    cos_table, sin_table = rope_tables(positions)
    head_shape = (group_rows, heads_here, HEAD_DIM)
    flat_shape = (group_rows, heads_here * HEAD_DIM)
    seq_shape = (sequences, SEQ_LEN, heads_here, HEAD_DIM)
    queries = (
        rotate(projected[0].reshape(head_shape), cos_table, sin_table)
        .astype(jnp.bfloat16)
        .reshape(seq_shape)
    )
    key_rows = (
        rotate(projected[1].reshape(head_shape), cos_table, sin_table)
        .astype(jnp.bfloat16)
        .reshape(seq_shape)
    )
    value_rows = projected[2].astype(jnp.bfloat16).reshape(seq_shape)
    seg_seq = segment_ids.reshape(sequences, SEQ_LEN)
    keep_seq = valid.reshape(sequences, SEQ_LEN)
    mixture, log_sums = lax.map(
        sequence_forward, (queries, key_rows, value_rows, seg_seq, keep_seq)
    )
    attended = mixture.reshape(flat_shape).astype(jnp.bfloat16)
    attn_branch = lax.psum_scatter(
        jnp.einsum("tc,dc->td", attended, out_local, preferred_element_type=jnp.float32),
        "tensor",
        scatter_dimension=0,
        tiled=True,
    )
    resid_own = hidden_f + attn_branch
    second_norm = layer_norm(resid_own, gain_rows[1]).astype(jnp.bfloat16)
    second_all = lax.all_gather(second_norm, "tensor", axis=0, tiled=True)
    gate_up = jnp.einsum(
        "td,kdf->ktf", second_all, gate_up_local, preferred_element_type=jnp.float32
    )
    gated_vals, gated_back = jax.vjp(gelu_gate, gate_up[0], gate_up[1])
    activated = gated_vals.astype(jnp.bfloat16)
    mlp_branch = lax.psum_scatter(
        jnp.einsum("tf,df->td", activated, down_local, preferred_element_type=jnp.float32),
        "tensor",
        scatter_dimension=0,
        tiled=True,
    )
    result = resid_own + mlp_branch
    output = result.astype(jnp.bfloat16)
    keep_own = lax.dynamic_slice_in_dim(valid, offset, own_rows, 0).astype(jnp.float32)[:, None]
    stat_terms = jnp.stack(
        [
            jnp.sum(keep_own),
            jnp.sum(keep_own * attn_branch * attn_branch),
            jnp.sum(keep_own * resid_own * resid_own),
            jnp.sum(keep_own * mlp_branch * mlp_branch),
            jnp.sum(keep_own * result * result),
        ]
    )
    stat_sums = lax.psum(stat_terms, ("dp", "tensor"))
    grad_all = lax.all_gather(out_grad, "tensor", axis=0, tiled=True)
    hidden_grad = jnp.einsum("td,df->tf", grad_all, down_local, preferred_element_type=jnp.float32)
    down_wgrad = jnp.einsum("td,tf->df", grad_all, activated, preferred_element_type=jnp.float32)
    gate_grad, up_grad = gated_back(hidden_grad)
    gate_up_grad = jnp.stack([gate_grad, up_grad]).astype(jnp.bfloat16)
    gate_up_wgrad = jnp.einsum(
        "td,ktf->kdf", second_all, gate_up_grad, preferred_element_type=jnp.float32
    )
    second_grad = lax.psum_scatter(
        jnp.einsum("ktf,kdf->td", gate_up_grad, gate_up_local, preferred_element_type=jnp.float32),
        "tensor",
        scatter_dimension=0,
        tiled=True,
    )
    norm_two_out, norm_two_back = jax.vjp(layer_norm, resid_own, gain_rows[1])
    resid_part, gain_two_grad = norm_two_back(second_grad)
    resid_grad = out_grad.astype(jnp.float32) + resid_part
    resid_grad_all = lax.all_gather(resid_grad.astype(jnp.bfloat16), "tensor", axis=0, tiled=True)
    mixed_grad = jnp.einsum(
        "td,dc->tc", resid_grad_all, out_local, preferred_element_type=jnp.float32
    ).astype(jnp.bfloat16)
    out_wgrad = jnp.einsum(
        "td,tc->dc", resid_grad_all, attended, preferred_element_type=jnp.float32
    )
    query_grad, key_grad, value_grad = lax.map(
        sequence_backward,
        (queries, key_rows, value_rows, seg_seq, keep_seq, log_sums, mixed_grad.reshape(seq_shape)),
    )
    qkv_grad = jnp.stack(
        [
            rotate_back(query_grad.reshape(head_shape), cos_table, sin_table).reshape(flat_shape),
            rotate_back(key_grad.reshape(head_shape), cos_table, sin_table).reshape(flat_shape),
            value_grad.reshape(flat_shape),
        ]
    ).astype(jnp.bfloat16)
    qkv_wgrad = jnp.einsum("td,ktc->kdc", first_all, qkv_grad, preferred_element_type=jnp.float32)
    first_grad = lax.psum_scatter(
        jnp.einsum("ktc,kdc->td", qkv_grad, qkv_local, preferred_element_type=jnp.float32),
        "tensor",
        scatter_dimension=0,
        tiled=True,
    )
    norm_one_out, norm_one_back = jax.vjp(layer_norm, hidden_f, gain_rows[0])
    input_part, gain_one_grad = norm_one_back(first_grad)
    input_grad = (resid_grad + input_part).astype(jnp.bfloat16)
    attn_part = to_owner(jnp.concatenate([qkv_wgrad, out_wgrad[None]], axis=0), owner_rows, owners)
    mlp_part = to_owner(
        jnp.concatenate([gate_up_wgrad, down_wgrad[None]], axis=0), owner_rows, owners
    )
    attn_grad, mlp_grad = (
        lax.psum_scatter(attn_part, "dp", scatter_dimension=1, tiled=True),
        lax.psum_scatter(mlp_part, "dp", scatter_dimension=1, tiled=True),
    )
    gain_part = jnp.stack([gain_one_grad, gain_two_grad])
    gain_grad = lax.psum(gain_part, ("dp", "tensor"))
    step_count = step.astype(jnp.float32)
    step_size = (
        learn_rate
        * jnp.sqrt(1.0 - jnp.power(beta_second, step_count))
        / (1.0 - jnp.power(beta_first, step_count))
    )
    attn_first_new, attn_second_new, attn_update, attn_scale = soap_block(
        attn_grad,
        attn_first,
        attn_second,
        attn_left,
        attn_right,
        step_size,
        beta_first,
        beta_second,
    )
    mlp_first_new, mlp_second_new, mlp_update, mlp_scale = soap_block(
        mlp_grad, mlp_first, mlp_second, mlp_left, mlp_right, step_size, beta_first, beta_second
    )
    gain_first_new = beta_first * gain_first + (1.0 - beta_first) * gain_grad
    gain_second_new = beta_second * gain_second + (1.0 - beta_second) * gain_grad * gain_grad
    gain_update = -step_size * gain_first_new / (jnp.sqrt(gain_second_new) + ADAM_EPS)
    root_means = jnp.sqrt(stat_sums[1:] / (stat_sums[0] * D))
    norm_scale = jnp.concatenate([attn_scale, mlp_scale], axis=0).reshape(7, 1, 1)
    return (
        output,
        input_grad,
        attn_grad,
        mlp_grad,
        gain_grad,
        attn_first_new,
        attn_second_new,
        mlp_first_new,
        mlp_second_new,
        gain_first_new,
        gain_second_new,
        attn_update,
        mlp_update,
        gain_update,
        norm_scale,
        root_means,
    )


def solution(mesh):
    return jax.shard_map(
        per_device,
        mesh=mesh,
        in_specs=(
            P(("dp", "tensor"), None),
            P(("dp", "tensor"), None),
            P(None, "dp", "tensor"),
            P(None, "dp", "tensor"),
            P(),
            P(None, "dp", "tensor"),
            P(None, "dp", "tensor"),
            P(None, "dp", "tensor"),
            P(None, "dp", "tensor"),
            P(None, "dp", "tensor"),
            P(None, "dp", "tensor"),
            P(None, "dp", "tensor"),
            P(None, "dp", "tensor"),
            P(),
            P(),
            P(),
            P("dp"),
            P("dp"),
            P("dp"),
            P(),
            P(),
            P(),
            P(),
        ),
        out_specs=(
            P(("dp", "tensor"), None),
            P(("dp", "tensor"), None),
            P(None, "dp", "tensor"),
            P(None, "dp", "tensor"),
            P(),
            P(None, "dp", "tensor"),
            P(None, "dp", "tensor"),
            P(None, "dp", "tensor"),
            P(None, "dp", "tensor"),
            P(),
            P(),
            P(None, "dp", "tensor"),
            P(None, "dp", "tensor"),
            P(),
            P(None, "dp", "tensor"),
            P(),
        ),
        check_vma=False,
    )
```

profile of v0, /device:TPU:0, one launch (start us, length us, event | category | flops | bytes accessed | tf_op | source)
XLA Modules:
  0.0 1532.7 jit_solution(12198340850637608766)
XLA Ops:
  20.2 20.3 %all-gather.7.cloned.1.call-done = bf16[4,1024,256]{2,1,0:T(8,128)(2,1)} async-done(((bf16[4,128,256]{2,1,0:T(8,128)(2,1)}), bf16[4,1024,256]{2,1,0:T(8,128)(2,1)}) %all-gather.7.cloned.1.call-update) | async-done | bytes 2097168 | tf_op jit(solution)/shard_map/all_gather | solution.py:212
  48.5 74.9 %all-gather.9.cloned.1.call-done = bf16[2048,1024]{1,0:T(8,128)(2,1)} async-done(((bf16[512,1024]{1,0:T(8,128)(2,1)}), bf16[2048,1024]{1,0:T(8,128)(2,1)}) %all-gather.9.cloned.1.call-update) | async-done | bytes 4194320 | tf_op jit(solution)/shard_map/all_gather | solution.py:226
  123.4 5.3 fusion.123
  143.2 51.9 %while.60 = (s32[]{:T(128)}, bf16[2,1024,4,64]{3,2,1,0:T(4,128)(2,1)}, f32[2,2,4,512]{3,2,1,0:T(4,128)S(1)}, bf16[2,1024,4,64]{1,3,2,0:T(8,128)(2,1)}, s32[2,102...) while((s32[]{:T(128)}, ...), condition=%wide.region_8.9_spmd.clone, body=%wide.region_3.8_spmd.sunk.clone | while | flops 564133376 | bytes 41292332 | solution.py:245
  146.5 19.8 %while.59 = (s32[]{:T(128)}, bf16[2,512,4,64]{1,3,2,0:T(8,128)(2,1)}, f32[2,4,512]{2,1,0:T(4,128)S(1)}, s32[2]{0:T(128)S(1)}, s32[1024]{0:T(1024)S(1)}, /*index=...) while((s32[]{:T(128)}, ...), condition=%wide.region_7.7_spmd, body=%wide.region_4.6_spmd.sunk | while | flops 564133376 | bytes 35475748 | solution.py:98
  172.3 19.8 %while.59 = (s32[]{:T(128)}, bf16[2,512,4,64]{1,3,2,0:T(8,128)(2,1)}, f32[2,4,512]{2,1,0:T(4,128)S(1)}, s32[2]{0:T(128)S(1)}, s32[1024]{0:T(1024)S(1)}, /*index=...) while((s32[]{:T(128)}, ...), condition=%wide.region_7.7_spmd, body=%wide.region_4.6_spmd.sunk | while | flops 564133376 | bytes 35475748 | solution.py:98
  199.0 5.6 fusion.220
  205.3 142.6 %reduce-scatter.7.cloned.1.call-done = f32[512,1024]{1,0:T(8,128)} async-done(((f32[2048,1024]{1,0:T(8,128)}), f32[512,1024]{1,0:T(8,128)}) %reduce-scatter.7.cloned.1.call-update) | async-done | bytes 2097168 | tf_op jit(solution)/shard_map/reduce_scatter | solution.py:249
  352.4 34.5 %all-gather.11.cloned.1.call-done = bf16[3,1024,656]{1,2,0:T(8,128)(2,1)} async-done(((bf16[3,128,656]{1,2,0:T(8,128)(2,1)}), bf16[3,1024,656]{1,2,0:T(8,128)(2,1)}) %all-gather.11.cloned.1.call-update) | async-done | bytes 4030480 | tf_op jit(solution)/shard_map/all_gather | solution.py:213
  391.7 5.2 gather_fusion.1
  403.3 66.4 %all-gather.13.cloned.1.call-done = bf16[2048,1024]{1,0:T(8,128)(2,1)} async-done(((bf16[512,1024]{1,0:T(8,128)(2,1)}), bf16[2048,1024]{1,0:T(8,128)(2,1)}) %all-gather.13.cloned.1.call-update) | async-done | bytes 4194320 | tf_op jit(solution)/shard_map/all_gather | solution.py:257
  469.7 8.9 convolution_bitcast_fusion
  482.5 16.6 %fusion.135 = f32[2048,1024]{1,0:T(8,128)} fusion(f32[2,2048,656]{1,2,0:T(8,128)S(1)} %convolution_bitcast_fusion, bf16[82,8,8,128]{3,2,1,0:T(8,128)(2,1)S(1)} %bitcast.412), kind=kOutput, calls=%fused_computation.177 | convolution fusion | flops 2840133632 | bytes 20480000 | tf_op jit(solution)/shard_map/tf,df->td/dot_general | solution.py:264
  499.2 51.2 %all-gather.15.cloned.1.call-done = bf16[2048,1024]{1,0:T(8,128)(2,1)} async-done(((bf16[512,1024]{1,0:T(8,128)(2,1)}), bf16[2048,1024]{1,0:T(8,128)(2,1)}) %all-gather.15.cloned.1.call-update) | async-done | bytes 4194320 | tf_op jit(solution)/shard_map/all_gather | solution.py:282
  550.4 5.3 fusion.160
  555.7 16.1 %fusion.138 = (bf16[1,2048,656]{1,2,0:T(8,128)(2,1)}, f32[2048,656]{0,1:T(8,128)S(1)}) fusion(f32[2,2048,656]{1,2,0:T(8,128)} %copy-done.4, f32[656,2048]{1,0:T(8,128)S(1)} %fusion.160), kind=kLoop, calls=%fused_computation.179 | loop fusion | flops 98074624 | bytes 24182784 | tf_op jit(solution)/shard_map/stack | solution.py:286
  571.8 9.6 fusion.130
  581.4 10.8 convolution_bitcast_fusion.2
  593.6 102.3 %reduce-scatter.9.cloned.1.call-done = f32[512,1024]{1,0:T(8,128)} async-done(((f32[2048,1024]{1,0:T(8,128)}), f32[512,1024]{1,0:T(8,128)}) %reduce-scatter.9.cloned.1.call-update) | async-done | bytes 2097168 | tf_op jit(solution)/shard_map/reduce_scatter | solution.py:263
  695.9 147.6 %reduce-scatter.11.cloned.1.call-done = f32[512,1024]{1,0:T(8,128)} async-done(((f32[2048,1024]{1,0:T(8,128)}), f32[512,1024]{1,0:T(8,128)}) %reduce-scatter.11.cloned.1.call-update) | async-done | bytes 2097168 | tf_op jit(solution)/shard_map/reduce_scatter | solution.py:290
  843.5 5.5 fusion.153
  855.0 9.9 fusion.157
  868.7 5.8 fusion.139
  878.8 7.6 gather_fusion.3
  886.4 7.7 bitcast_select_fusion
  894.1 39.8 %all-gather.17.cloned.1.call-done = bf16[2048,1024]{1,0:T(8,128)(2,1)} async-done(((bf16[512,1024]{1,0:T(8,128)(2,1)}), bf16[2048,1024]{1,0:T(8,128)(2,1)}) %all-gather.17.cloned.1.call-update) | async-done | bytes 4194320 | tf_op jit(solution)/shard_map/all_gather | solution.py:299
  944.2 270.1 %while.62 = (s32[]{:T(128)}, f32[2,1024,4,64]{3,2,1,0:T(4,128)}, f32[2,1024,4,64]{1,0,3,2:T(2,128)}, bf16[2,1024,4,64]{1,3,2,0:T(8,128)(2,1)}, bf16[2,1024,4,64]...) while((s32[]{:T(128)}, f32[2,1024,4,64]{3,2,1,0:T(4,128)}, ...), condition=%wide.region_20.21_spmd.clone, body=%wide.region_16.20_spmd.sunk.clone | while | flops 1399856640 | bytes 152171168 | solution.py:306
  948.7 104.8 %while.61 = (s32[]{:T(128)}, f32[1024,4,64]{0,2,1:T(8,128)}, f32[1024,4,64]{0,2,1:T(8,128)}, f32[2,512,4,64]{1,3,2,0:T(8,128)}, s32[2]{0:T(128)S(1)}, /*index=5*...) while((s32[]{:T(128)}, f32[1024,4,64]{0,2,1:T(8,128)}, ...), condition=%wide.region_19.19_spmd.clone, body=%wide.region_17.18_spmd.clone.sunk | while | flops 1399856640 | bytes 136393040 | solution.py:138
  963.2 19.3 %fusion.289 = f32[1024,4,64]{0,2,1:T(8,128)} fusion(f32[4,512,1024]{2,1,0:T(8,128)} %fusion.286, f32[4,512,1024]{2,1,0:T(8,128)} %copy-done.1, f32[4,512]{1,0:T(4,128)S(1)} %dynamic-slice_bitcast_fusion.20, pred[512,1024]{1,0:T(8,128)(4,1)S(1)} %fusion.288, f32[1024,4,64]{0,2,1:T(8,128)} %get-tuple-element.967, pred[]{:T(512)S(6)} %compare.3, ...), kind=kOutput, calls=%fused_computation.53.clone.1 | convolution fusion | flops 292031488 | bytes 36978692 | tf_op jit(solution)/shard_map/while/body/eval_jaxpr/while/body/eval_jaxpr/hqk,qhe->khe/dot_general | solution.py:129
  982.6 18.0 %fusion.291 = f32[2,512,4,64]{1,3,2,0:T(8,128)} fusion(f32[2,512,4,64]{1,3,2,0:T(8,128)} %get-tuple-element.969, s32[]{:T(128)S(6)} %copy.252, bf16[1024,4,64]{0,2,1:T(8,128)(2,1)S(1)} %get-tuple-element.991, f32[4,512,1024]{2,1,0:T(8,128)} %fusion.286, f32[4,512,1024]{2,1,0:T(8,128)} %copy-done.1, f32[4,512]{1,0:T(4,128)S(1)} %dynamic-slice_bitcast_fusion.20, ...), kind=kOutput, calls=%fused_computation.56.clone.1 | convolution fusion | flops 291507200 | bytes 35667972 | tf_op jit(solution)/shard_map/while/body/eval_jaxpr/while/body/eval_jaxpr/hqk,khe->qhe/dot_general | solution.py:126
  1016.4 19.2 %fusion.289 = f32[1024,4,64]{0,2,1:T(8,128)} fusion(f32[4,512,1024]{2,1,0:T(8,128)} %fusion.286, f32[4,512,1024]{2,1,0:T(8,128)} %copy-done.1, f32[4,512]{1,0:T(4,128)S(1)} %dynamic-slice_bitcast_fusion.20, pred[512,1024]{1,0:T(8,128)(4,1)S(1)} %fusion.288, f32[1024,4,64]{0,2,1:T(8,128)} %get-tuple-element.967, pred[]{:T(512)S(6)} %compare.3, ...), kind=kOutput, calls=%fused_computation.53.clone.1 | convolution fusion | flops 292031488 | bytes 36978692 | tf_op jit(solution)/shard_map/while/body/eval_jaxpr/while/body/eval_jaxpr/hqk,qhe->khe/dot_general | solution.py:129
  1035.6 17.9 %fusion.291 = f32[2,512,4,64]{1,3,2,0:T(8,128)} fusion(f32[2,512,4,64]{1,3,2,0:T(8,128)} %get-tuple-element.969, s32[]{:T(128)S(6)} %copy.252, bf16[1024,4,64]{0,2,1:T(8,128)(2,1)S(1)} %get-tuple-element.991, f32[4,512,1024]{2,1,0:T(8,128)} %fusion.286, f32[4,512,1024]{2,1,0:T(8,128)} %copy-done.1, f32[4,512]{1,0:T(4,128)S(1)} %dynamic-slice_bitcast_fusion.20, ...), kind=kOutput, calls=%fused_computation.56.clone.1 | convolution fusion | flops 291507200 | bytes 35667972 | tf_op jit(solution)/shard_map/while/body/eval_jaxpr/while/body/eval_jaxpr/hqk,khe->qhe/dot_general | solution.py:126
  1055.8 18.7 %dynamic_update_slice.56 = f32[2,1024,4,64]{1,0,3,2:T(2,128)} dynamic-update-slice(f32[2,1024,4,64]{1,0,3,2:T(2,128)} %get-tuple-element.1054, f32[1,1024,4,64]{1,0,3,2:T(1,128)S(1)} %copy.233, s32[]{:T(128)S(6)} %copy.276, s32[]{:T(128)} %constant.121.clone.1..sunk.6, s32[]{:T(128)} %constant.121.clone.1..sunk.6, s32[]{:T(128)} %constant.121.clone.1..sunk.6) | dynamic-update-slice | bytes 2097156 | tf_op jit(solution)/shard_map/while/body/jit(dynamic_update_index_in_dim)/dynamic_update_slice | solution.py:245
  1083.4 104.2 %while.61 = (s32[]{:T(128)}, f32[1024,4,64]{0,2,1:T(8,128)}, f32[1024,4,64]{0,2,1:T(8,128)}, f32[2,512,4,64]{1,3,2,0:T(8,128)}, s32[2]{0:T(128)S(1)}, /*index=5*...) while((s32[]{:T(128)}, f32[1024,4,64]{0,2,1:T(8,128)}, ...), condition=%wide.region_19.19_spmd.clone, body=%wide.region_17.18_spmd.clone.sunk | while | flops 1399856640 | bytes 136393040 | solution.py:138
  1097.9 19.0 %fusion.289 = f32[1024,4,64]{0,2,1:T(8,128)} fusion(f32[4,512,1024]{2,1,0:T(8,128)} %fusion.286, f32[4,512,1024]{2,1,0:T(8,128)} %copy-done.1, f32[4,512]{1,0:T(4,128)S(1)} %dynamic-slice_bitcast_fusion.20, pred[512,1024]{1,0:T(8,128)(4,1)S(1)} %fusion.288, f32[1024,4,64]{0,2,1:T(8,128)} %get-tuple-element.967, pred[]{:T(512)S(6)} %compare.3, ...), kind=kOutput, calls=%fused_computation.53.clone.1 | convolution fusion | flops 292031488 | bytes 36978692 | tf_op jit(solution)/shard_map/while/body/eval_jaxpr/while/body/eval_jaxpr/hqk,qhe->khe/dot_general | solution.py:129
  1116.9 17.9 %fusion.291 = f32[2,512,4,64]{1,3,2,0:T(8,128)} fusion(f32[2,512,4,64]{1,3,2,0:T(8,128)} %get-tuple-element.969, s32[]{:T(128)S(6)} %copy.252, bf16[1024,4,64]{0,2,1:T(8,128)(2,1)S(1)} %get-tuple-element.991, f32[4,512,1024]{2,1,0:T(8,128)} %fusion.286, f32[4,512,1024]{2,1,0:T(8,128)} %copy-done.1, f32[4,512]{1,0:T(4,128)S(1)} %dynamic-slice_bitcast_fusion.20, ...), kind=kOutput, calls=%fused_computation.56.clone.1 | convolution fusion | flops 291507200 | bytes 35667972 | tf_op jit(solution)/shard_map/while/body/eval_jaxpr/while/body/eval_jaxpr/hqk,khe->qhe/dot_general | solution.py:126
  1150.6 19.2 %fusion.289 = f32[1024,4,64]{0,2,1:T(8,128)} fusion(f32[4,512,1024]{2,1,0:T(8,128)} %fusion.286, f32[4,512,1024]{2,1,0:T(8,128)} %copy-done.1, f32[4,512]{1,0:T(4,128)S(1)} %dynamic-slice_bitcast_fusion.20, pred[512,1024]{1,0:T(8,128)(4,1)S(1)} %fusion.288, f32[1024,4,64]{0,2,1:T(8,128)} %get-tuple-element.967, pred[]{:T(512)S(6)} %compare.3, ...), kind=kOutput, calls=%fused_computation.53.clone.1 | convolution fusion | flops 292031488 | bytes 36978692 | tf_op jit(solution)/shard_map/while/body/eval_jaxpr/while/body/eval_jaxpr/hqk,qhe->khe/dot_general | solution.py:129
  1169.8 17.9 %fusion.291 = f32[2,512,4,64]{1,3,2,0:T(8,128)} fusion(f32[2,512,4,64]{1,3,2,0:T(8,128)} %get-tuple-element.969, s32[]{:T(128)S(6)} %copy.252, bf16[1024,4,64]{0,2,1:T(8,128)(2,1)S(1)} %get-tuple-element.991, f32[4,512,1024]{2,1,0:T(8,128)} %fusion.286, f32[4,512,1024]{2,1,0:T(8,128)} %copy-done.1, f32[4,512]{1,0:T(4,128)S(1)} %dynamic-slice_bitcast_fusion.20, ...), kind=kOutput, calls=%fused_computation.56.clone.1 | convolution fusion | flops 291507200 | bytes 35667972 | tf_op jit(solution)/shard_map/while/body/eval_jaxpr/while/body/eval_jaxpr/hqk,khe->qhe/dot_general | solution.py:126
  1190.0 18.7 %dynamic_update_slice.56 = f32[2,1024,4,64]{1,0,3,2:T(2,128)} dynamic-update-slice(f32[2,1024,4,64]{1,0,3,2:T(2,128)} %get-tuple-element.1054, f32[1,1024,4,64]{1,0,3,2:T(1,128)S(1)} %copy.233, s32[]{:T(128)S(6)} %copy.276, s32[]{:T(128)} %constant.121.clone.1..sunk.6, s32[]{:T(128)} %constant.121.clone.1..sunk.6, s32[]{:T(128)} %constant.121.clone.1..sunk.6) | dynamic-update-slice | bytes 2097156 | tf_op jit(solution)/shard_map/while/body/jit(dynamic_update_index_in_dim)/dynamic_update_slice | solution.py:245
  1222.4 6.5 copy.174
  1228.9 7.8 fusion.218
  1250.1 8.4 fusion.154
  1278.6 7.6 convolution_bitcast_fusion.1
  1291.8 13.7 multiply_reduce_fusion.5
  1306.9 5.3 multiply_reduce_fusion.4
  1316.6 11.6 reduce-scatter.15.cloned.1.call-done
  1335.5 139.6 %reduce-scatter.13.cloned.1.call-done = f32[512,1024]{1,0:T(8,128)} async-done(((f32[2048,1024]{1,0:T(8,128)}), f32[512,1024]{1,0:T(8,128)}) %reduce-scatter.13.cloned.1.call-update) | async-done | bytes 2097168 | tf_op jit(solution)/shard_map/reduce_scatter | solution.py:318
  1479.8 41.0 %all-reduce = (f32[2,1024]{1,0:T(2,128)S(1)}, f32[5]{0:T(128)S(1)}) all-reduce(f32[2,1024]{1,0:T(2,128)S(1)} %pad_maximum_fusion.14, f32[5]{0:T(128)S(1)} %stack.49), channel_id=1, replica_groups=mesh['dp'=8,'tensor'=4] {'dp','tensor'}, use_global_device_ids=true, to_apply=%region_28.29 | all-reduce | flops 2053 | bytes 16424 | tf_op jit(solution)/shard_map/psum | solution.py:336
  (415 shorter events, 272.7 us)
Async XLA Ops:
  7.2 1322.7 %copy-start = (f32[4,256,256]{2,1,0:T(8,128)S(1)}, f32[4,256,256]{2,1,0:T(8,128)}, u32[]{:S(2)}) copy-start(f32[4,256,256]{2,1,0:T(8,128)} %param.39) | copy-start | bytes 3145732
  7.2 33.2 %all-gather.7.cloned.1.call-start = ((), (), s32[]{:S(2)}) async-start(), calls=%async_computation.6 | async-start | bytes 2359296 | tf_op jit(solution)/shard_map/all_gather | solution.py:212
  8.0 115.4 %all-gather.9.cloned.1.call-start = ((), (), s32[]{:S(2)}) async-start(), calls=%async_computation.7 | async-start | bytes 5242880 | tf_op jit(solution)/shard_map/all_gather | solution.py:226
  16.3 331.7 %reduce-scatter.7.cloned.1.call-start = ((), (), s32[]{:S(2)}) async-start(), calls=%async_computation.8 | async-start | bytes 10485760 | tf_op jit(solution)/shard_map/reduce_scatter | solution.py:249
  16.5 26.5 %copy-start.65 = (s32[1024]{0:T(1024)}, s32[1024]{0:T(1024)S(1)}, u32[]{:S(2)}) copy-start(s32[1024]{0:T(1024)S(1)} %pad_clamp_fusion.1) | copy-start | bytes 12292
  18.4 25.6 %copy-start.68 = (pred[8]{0:T(512)(128)(4,1)}, pred[8]{0:T(512)(128)(4,1)S(1)}, u32[]{:S(2)}) copy-start(pred[8]{0:T(512)(128)(4,1)S(1)} %compare_and_fusion.1) | copy-start | bytes 28
  20.2 108.9 %copy-start.20 = (f32[2048,32]{0,1:T(8,128)}, f32[2048,32]{0,1:T(8,128)S(1)}, u32[]{:S(2)}) copy-start(f32[2048,32]{0,1:T(8,128)S(1)} %get-tuple-element.492) | copy-start | bytes 786436
  48.5 74.9 %copy-start.25 = (bf16[3,1024,256]{1,2,0:T(8,128)(2,1)}, bf16[3,1024,256]{1,2,0:T(8,128)(2,1)S(1)}, u32[]{:S(2)}) copy-start(bf16[3,1024,256]{1,2,0:T(8,128)(2,1)S(1)} %slice.75) | copy-start | bytes 4718596
  195.1 9.5 copy-start.3
  195.1 9.5 copy-start.38
  195.1 9.5 copy-start.40
  195.1 9.5 copy-start.43
  204.7 145.8 %copy-start.50 = (f32[1,1024]{1,0:T(1,128)S(1)}, f32[1,1024]{1,0:T(1,128)}, u32[]{:S(2)}) copy-start(f32[1,1024]{1,0:T(1,128)} %get-tuple-element.494) | copy-start | bytes 12292
  204.7 182.2 %all-gather.11.cloned.1.call-start = ((), (), s32[]{:S(2)}) async-start(), calls=%async_computation.9 | async-start | bytes 4534272 | tf_op jit(solution)/shard_map/all_gather | solution.py:213
  205.3 264.4 %all-gather.13.cloned.1.call-start = ((), (), s32[]{:S(2)}) async-start(), calls=%async_computation.10 | async-start | bytes 5242880 | tf_op jit(solution)/shard_map/all_gather | solution.py:257
  351.8 198.6 %all-gather.15.cloned.1.call-start = ((), (), s32[]{:S(2)}) async-start(), calls=%async_computation.12 | async-start | bytes 5242880 | tf_op jit(solution)/shard_map/all_gather | solution.py:282
  352.4 343.5 %reduce-scatter.9.cloned.1.call-start = ((), (), s32[]{:S(2)}) async-start(), calls=%async_computation.11 | async-start | bytes 10485760 | tf_op jit(solution)/shard_map/reduce_scatter | solution.py:263
  469.7 12.8 copy-start.27
  499.1 344.4 %reduce-scatter.11.cloned.1.call-start = ((), (), s32[]{:S(2)}) async-start(), calls=%async_computation.13 | async-start | bytes 10485760 | tf_op jit(solution)/shard_map/reduce_scatter | solution.py:290
  555.7 16.1 %copy-start.6 = (f32[656,2048]{1,0:T(8,128)}, f32[656,2048]{1,0:T(8,128)S(1)}, u32[]{:S(2)}) copy-start(f32[656,2048]{1,0:T(8,128)S(1)} %fusion.160) | copy-start | bytes 16121860
  571.8 9.6 copy-start.5
  571.8 9.6 copy-start.17
  592.2 341.7 %all-gather.17.cloned.1.call-start = ((), (), s32[]{:S(2)}) async-start(), calls=%async_computation.14 | async-start | bytes 5242880 | tf_op jit(solution)/shard_map/all_gather | solution.py:299
  852.4 436.9 %reduce-scatter.17.cloned.1.call-start = ((), (), s32[]{:S(2)}) async-start(), calls=%async_computation.17 | async-start | bytes 9068544 | tf_op jit(solution)/shard_map/reduce_scatter | solution.py:333
  852.5 26.2 %copy-start.64 = (s32[1024]{0:T(1024)}, s32[1024]{0:T(1024)S(1)}, u32[]{:S(2)}) copy-start(s32[1024]{0:T(1024)S(1)} %pad_clamp_fusion) | copy-start | bytes 12292
  852.6 33.7 %copy-start.66 = (pred[1024]{0:T(1024)(128)(4,1)}, pred[1024]{0:T(1024)(128)(4,1)S(1)}, u32[]{:S(2)}) copy-start(pred[1024]{0:T(1024)(128)(4,1)S(1)} %broadcast_bitcast_fusion) | copy-start | bytes 3076
  894.0 39.9 %copy-start.23 = (bf16[1,8,128,256]{3,2,0,1:T(8,128)(2,1)S(1)}, bf16[1,8,128,256]{3,2,0,1:T(8,128)(2,1)}, u32[]{:S(2)}) copy-start(bf16[1,8,128,256]{3,2,0,1:T(8,128)(2,1)} %slice.114) | copy-start | bytes 1572868
  894.0 50.1 %copy-start.39 = (s32[2,1024]{1,0:T(2,128)S(1)}, s32[2,1024]{1,0:T(2,128)}, u32[]{:S(2)}) copy-start(s32[2,1024]{1,0:T(2,128)} %copy-done.38) | copy-start | bytes 24580
  894.0 50.1 %copy-start.41 = (s32[2,1024]{1,0:T(2,128)S(1)}, s32[2,1024]{1,0:T(2,128)}, u32[]{:S(2)}) copy-start(s32[2,1024]{1,0:T(2,128)} %copy-done.40) | copy-start | bytes 24580
  894.1 50.1 %copy-start.44 = (f32[2,2,4,512]{3,2,1,0:T(4,128)S(1)}, f32[2,2,4,512]{3,2,1,0:T(4,128)}, u32[]{:S(2)}) copy-start(f32[2,2,4,512]{3,2,1,0:T(4,128)} %copy-done.43) | copy-start | bytes 98308
  894.1 434.2 %reduce-scatter.15.cloned.1.call-start = ((), (), s32[]{:S(2)}) async-start(), calls=%async_computation.16 | async-start | bytes 4718592 | tf_op jit(solution)/shard_map/reduce_scatter | solution.py:332
  1236.7 9.2 copy-start.21
  1278.5 196.6 %reduce-scatter.13.cloned.1.call-start = ((), (), s32[]{:S(2)}) async-start(), calls=%async_computation.15 | async-start | bytes 10485760 | tf_op jit(solution)/shard_map/reduce_scatter | solution.py:318
  1289.3 17.5 %slice-start = ((s8[6045696]{0:T(1024)(128)(4,1)}), s8[4194304]{0:T(1024)(128)(4,1)S(1)}, s32[]{:S(2)}) async-start(s8[6045696]{0:T(1024)(128)(4,1)} %bitcast.391), calls=%async_computation.18 | async-start | bytes 8388608
  1291.7 15.1 slice-start.1
  1306.9 21.4 %copy-start.42 = (f32[4,128,128]{2,1,0:T(8,128)S(1)}, f32[4,128,128]{2,1,0:T(8,128)}, u32[]{:S(2)}) copy-start(f32[4,128,128]{2,1,0:T(8,128)} %param.38) | copy-start | bytes 786436
  1306.9 23.0 %copy-start.34 = (f32[4,128,256]{2,1,0:T(8,128)S(1)}, f32[4,128,256]{2,1,0:T(8,128)}, u32[]{:S(2)}) copy-start(f32[4,128,256]{2,1,0:T(8,128)} %param.37) | copy-start | bytes 1572868
  1306.9 23.0 %copy-start.35 = (f32[4,128,256]{2,1,0:T(8,128)S(1)}, f32[4,128,256]{2,1,0:T(8,128)}, u32[]{:S(2)}) copy-start(f32[4,128,256]{2,1,0:T(8,128)} %param.36) | copy-start | bytes 1572868
  1313.3 161.8 %copy-start.2 = (bf16[512,1024]{1,0:T(8,128)(2,1)S(1)}, bf16[512,1024]{1,0:T(8,128)(2,1)}, u32[]{:S(2)}) copy-start(bf16[512,1024]{1,0:T(8,128)(2,1)} %param.31) | copy-start | bytes 3145732
  1313.3 161.8 %copy-start.47 = (f32[1,1024]{1,0:T(1,128)S(1)}, f32[1,1024]{1,0:T(1,128)}, u32[]{:S(2)}) copy-start(f32[1,1024]{1,0:T(1,128)} %copy-done.46) | copy-start | bytes 12292
  1313.3 161.8 %copy-start.49 = (f32[512]{0:T(512)S(1)}, f32[512]{0:T(512)}, u32[]{:S(2)}) copy-start(f32[512]{0:T(512)} %copy-done.48) | copy-start | bytes 6148
  1329.9 147.2 %copy-start.56 = (f32[512]{0:T(512)S(1)}, f32[512]{0:T(512)}, u32[]{:S(2)}) copy-start(f32[512]{0:T(512)} %copy-done.55) | copy-start | bytes 6148
  1330.0 147.2 %copy-start.52 = (f32[512]{0:T(512)S(1)}, f32[512]{0:T(512)}, u32[]{:S(2)}) copy-start(f32[512]{0:T(512)} %copy-done.51) | copy-start | bytes 6148
  1331.9 147.8 %copy-start.57 = (f32[1024]{0:T(1024)S(1)}, f32[1024]{0:T(1024)}, u32[]{:S(2)}) copy-start(f32[1024]{0:T(1024)} %get-tuple-element.358) | copy-start | bytes 12292
  1331.9 189.5 %copy-start.59 = (f32[2,1024]{1,0:T(2,128)S(1)}, f32[2,1024]{1,0:T(2,128)}, u32[]{:S(2)}) copy-start(f32[2,1024]{1,0:T(2,128)} %param.45) | copy-start | bytes 24580
  1331.9 189.5 %copy-start.60 = (f32[2,1024]{1,0:T(2,128)S(1)}, f32[2,1024]{1,0:T(2,128)}, u32[]{:S(2)}) copy-start(f32[2,1024]{1,0:T(2,128)} %param.44) | copy-start | bytes 24580
  1331.9 190.1 %copy-start.14 = (bf16[512,1024]{1,0:T(8,128)(2,1)S(1)}, bf16[512,1024]{1,0:T(8,128)(2,1)}, u32[]{:S(2)}) copy-start(bf16[512,1024]{1,0:T(8,128)(2,1)} %param.32) | copy-start | bytes 3145732
  1331.9 190.1 %copy-start.54 = (f32[512]{0:T(512)S(1)}, f32[512]{0:T(512)}, u32[]{:S(2)}) copy-start(f32[512]{0:T(512)} %copy-done.53) | copy-start | bytes 6148
  (51 other events, 180.4 us)
Sparse Core Ops, SparseCore 0:
  10.0 30.4 all-gather.6
  42.6 80.7 all-gather.8
  204.8 143.0 reduce-scatter.6
  349.7 37.2 all-gather.10
  388.9 80.7 all-gather.12
  471.1 79.2 all-gather.14
  552.7 143.0 reduce-scatter.8
  698.2 145.2 reduce-scatter.10
  852.5 81.3 all-gather.16
  937.9 67.8 reduce-scatter.16
  1278.6 49.5 reduce-scatter.14
  1330.4 144.6 reduce-scatter.12
where the time goes:
time: 1550 us; the launch traced here: 1530 us
  waiting for transfers between devices  833 us (54%)
  matrix products  332 us (21%)
  local copies, waits for them, and re-layouts  192 us (12%)
  other arithmetic  102 us (7%)
  blocking collectives  41 us (3%)
  between operations  18.7 us (1%)
    reduce_scatter x1, waiting for transfers between devices, per_device(): lax.psum_scatter(jnp.einsum('ktf,kdf->td', gate_up_grad, gate_up_local, p...  148 us
    reduce_scatter x1, waiting for transfers between devices, per_device(): lax.psum_scatter(jnp.einsum('tc,dc->td', attended, out_local, preferred_e...  143 us
    reduce_scatter x1, waiting for transfers between devices, per_device(): lax.psum_scatter(jnp.einsum('ktc,kdc->td', qkv_grad, qkv_local, preferred...  140 us
    reduce_scatter x1, waiting for transfers between devices, per_device(): lax.psum_scatter(jnp.einsum('tf,df->td', activated, down_local, preferred...  102 us
    dot_general x4, matrix products, one_block(): jnp.einsum('hqk,qhe->khe', raw_grad, query_block, preferred_element_type=...  76.8 us
    all_gather x1, waiting for transfers between devices, per_device(): first_all = lax.all_gather(first_norm, 'tensor', axis=0, tiled=True)  74.9 us
    dot_general x4, matrix products, one_block(): jnp.einsum('hqk,khe->qhe', raw_grad, key_rows, preferred_element_type=jnp...  71.6 us
    all_gather x1, waiting for transfers between devices, per_device(): second_all = lax.all_gather(second_norm, 'tensor', axis=0, tiled=True)  66.4 us
  transfers between devices with their start and end apart: 12, of which 11 were waited for; matrix products, arithmetic and copies ran while one was open for 34% of the time, Pallas kernels for 0%

commit v1 on v0

v1 whole, which is shorter than its diff:
```python
import functools
import math

import jax
import jax.numpy as jnp
from jax import lax
from jax.experimental import pallas as pl
from jax.experimental.pallas import tpu as pltpu
from jax.sharding import PartitionSpec as P

D = 1024
HEADS = 16
HEAD_DIM = 64
SEQ_LEN = 1024
NORM_EPS = 1e-05
ROPE_BASE = 160000.0
ADAM_EPS = 1e-08
SCALE_EPS = 1e-06
PRECISE = lax.Precision.HIGHEST
F32 = jnp.float32
BF = jnp.bfloat16
AXES = ("dp", "tensor")
TN = (((0,), (0,)), ((), ()))

NT=(((1,),(1,)),((),()))
NN=(((1,),(0,)),((),()))
def dot(a,b,dims=NN):
    return lax.dot_general(a,b,dims,preferred_element_type=F32)

def swap_halves(x):
    lane=lax.broadcasted_iota(jnp.int32,x.shape,1)
    return jnp.where(lane%64<32,pltpu.roll(x,96,1),pltpu.roll(x,32,1))

def fwd_kernel(chunk,qraw,kraw,vraw,cosk,sink,segq,segk,keepk,o_ref,q_ref,k_ref,v_ref,p_ref,r_ref,bias):
    rows_q=qraw.shape[0]; rows_k=kraw.shape[0]
    @pl.when(pl.program_id(0)==0)
    def _():
        ki=lax.broadcasted_iota(jnp.int32,(rows_k,rows_q),0)
        qi=lax.broadcasted_iota(jnp.int32,(rows_k,rows_q),1)
        ok=(segk[...]==segq[...])&((keepk[...]>0)|(ki==qi))
        bias[...]=jnp.where(ok,0.0,-1e30)
    q32=qraw[...]; k32=kraw[...]
    q=(q32*cosk[:rows_q]+swap_halves(q32)*sink[:rows_q]).astype(BF)
    k=(k32*cosk[...]+swap_halves(k32)*sink[...]).astype(BF)
    q_ref[...]=q; k_ref[...]=k
    v32=vraw[...]
    v_ref[...]=v32.astype(BF)
    vt=v32.T.astype(BF)
    lane=lax.broadcasted_iota(jnp.int32,q.shape,1)
    row=lax.broadcasted_iota(jnp.int32,(128,1),0)
    qs=q*jnp.asarray(0.125,BF)
    parts=[]
    qh=[jnp.where(lane//64==h,qs,jnp.zeros_like(qs)) for h in range(2)]
    for c in range(rows_q//chunk):
        sl=slice(c*chunk,(c+1)*chunk)
        outs=[]
        for h in range(2):
            s=dot(k,qh[h][sl],NT)+bias[:,sl]
            m=jnp.max(s,axis=0,keepdims=True)
            p=jnp.exp(s-m)
            l=jnp.sum(p,axis=0,keepdims=True)
            pb=p.astype(BF)
            p_ref[h,:,sl]=pb
            r=1.0/l
            r_ref[0,h:h+1,sl]=r
            outs.append(dot(vt,pb)*r)
        parts.append(jnp.where(row<64,outs[0],outs[1]))
    ot=jnp.concatenate(parts,axis=1) if len(parts)>1 else parts[0]
    o_ref[...]=ot.T.astype(BF)

def attn_fwd(qraw,kraw,vraw,cosk,sink,segq,segk,keepk,chunk=512):
    rq,width=qraw.shape; rk=kraw.shape[0]; pairs=width//128
    chunk=min(chunk,rq)
    sd=jax.ShapeDtypeStruct
    col=lambda r:pl.BlockSpec((r,128),lambda i:(0,i))
    full=lambda a:pl.BlockSpec(a.shape,lambda i:(0,0))
    return pl.pallas_call(functools.partial(fwd_kernel,chunk),grid=(pairs,),
        in_specs=[col(rq),col(rk),col(rk),full(cosk),full(sink),full(segq),full(segk),full(keepk)],
        out_specs=[col(rq),col(rq),col(rk),col(rk),pl.BlockSpec((2,rk,rq),lambda i:(i,0,0)),pl.BlockSpec((1,2,rq),lambda i:(i,0,0))],
        out_shape=[sd((rq,width),BF),sd((rq,width),BF),sd((rk,width),BF),sd((rk,width),BF),sd((2*pairs,rk,rq),BF),sd((pairs,2,rq),F32)],
        scratch_shapes=[pltpu.VMEM((rk,rq),F32)],
        compiler_params=pltpu.CompilerParams(dimension_semantics=("arbitrary",),vmem_limit_bytes=60<<20),
        cost_estimate=pl.CostEstimate(flops=4*rq*rk*width,bytes_accessed=4*pairs*rk*rq+12*rk*width,transcendentals=2*pairs*rk*rq),
        name="attn_fwd")(qraw,kraw,vraw,cosk,sink,segq,segk,keepk)

def bwd_kernel(chunk,q_ref,k_ref,v_ref,o_ref,do_ref,p_ref,r_ref,cosk,sink,dq_ref,dk_ref,dv_ref):
    rows_q=q_ref.shape[0]
    q=q_ref[...]; k=k_ref[...]; v=v_ref[...]
    kt=k.astype(F32).T
    dot_t=do_ref[...].astype(F32).T
    o_t=o_ref[...].astype(F32).T
    row=lax.broadcasted_iota(jnp.int32,(128,1),0)
    lane=lax.broadcasted_iota(jnp.int32,(1,128),1)
    r=r_ref[0]
    dpt=dot_t*jnp.where(row<64,r[0:1],r[1:2])
    dprod=dpt*o_t
    dp_rows=dpt.T
    dk=jnp.zeros(k.shape,F32); dv=jnp.zeros(k.shape,F32)
    dqs=[]
    for c in range(rows_q//chunk):
        sl=slice(c*chunk,(c+1)*chunk)
        dqt=None
        for h in range(2):
            hs=slice(h*64,(h+1)*64)
            p=p_ref[h,:,sl]
            dh=jnp.where(row//64==h,dpt[:,sl],0.0).astype(BF)
            dp=dot(v,dh)
            delta=jnp.sum(dprod[hs,sl],axis=0,keepdims=True)
            ds=(p.astype(F32)*(dp-delta)).astype(BF)
            kh=jnp.where(row//64==h,kt,0.0).astype(BF)
            t=dot(kh,ds)
            dqt=t if dqt is None else dqt+t
            qh=jnp.where(lane//64==h,q[sl],jnp.zeros_like(q[sl]))
            dk=dk+dot(ds,qh)
            dh2=jnp.where(lane//64==h,dp_rows[sl],0.0).astype(BF)
            dv=dv+dot(p,dh2)
        dqs.append(dqt)
    dqt=jnp.concatenate(dqs,axis=1) if len(dqs)>1 else dqs[0]
    dq=dqt.T
    dq=(dq*cosk[:rows_q]-swap_halves(dq)*sink[:rows_q])*0.125
    dk=(dk*cosk[...]-swap_halves(dk)*sink[...])*0.125
    dq_ref[...]=dq.astype(BF); dk_ref[...]=dk.astype(BF); dv_ref[...]=dv.astype(BF)

def attn_bwd(q,k,v,o,do,p,r,cosk,sink,chunk=512):
    rq,width=q.shape; rk=k.shape[0]; pairs=width//128
    chunk=min(chunk,rq)
    sd=jax.ShapeDtypeStruct
    col=lambda n:pl.BlockSpec((n,128),lambda i:(0,i))
    full=lambda a:pl.BlockSpec(a.shape,lambda i:(0,0))
    return pl.pallas_call(functools.partial(bwd_kernel,chunk),grid=(pairs,),
        in_specs=[col(rq),col(rk),col(rk),col(rq),col(rq),pl.BlockSpec((2,rk,rq),lambda i:(i,0,0)),pl.BlockSpec((1,2,rq),lambda i:(i,0,0)),full(cosk),full(sink)],
        out_specs=[col(rq),col(rk),col(rk)],
        out_shape=[sd((rq,width),BF),sd((rk,width),BF),sd((rk,width),BF)],
        compiler_params=pltpu.CompilerParams(dimension_semantics=("arbitrary",),vmem_limit_bytes=60<<20),
        cost_estimate=pl.CostEstimate(flops=8*rq*rk*width,bytes_accessed=4*pairs*rk*rq+12*rk*width,transcendentals=0),
        name="attn_bwd")(q,k,v,o,do,p,r,cosk,sink)


def norm_stats(values):
    average = jnp.mean(values, axis=-1, keepdims=True)
    centred = values - average
    spread = jnp.mean(centred * centred, axis=-1, keepdims=True)
    scale = lax.rsqrt(spread + NORM_EPS)
    return centred * scale, scale


def norm_back(values, gain_row, grads):
    unit, scale = norm_stats(values)
    inner = grads * gain_row
    part = scale * (
        inner
        - jnp.mean(inner, axis=-1, keepdims=True)
        - unit * jnp.mean(inner * unit, axis=-1, keepdims=True)
    )
    return part, jnp.sum(grads * unit, axis=0)


def gather_rows(shards):
    count, rows, slab = shards.shape
    got = lax.all_gather(shards, AXES, axis=0, tiled=False)
    owners, shards_n = lax.axis_size("dp"), lax.axis_size("tensor")
    got = got.reshape(owners, shards_n, count, rows, slab).transpose(2, 1, 3, 0, 4)
    return got.reshape(count, shards_n * rows, owners * slab)


def scatter_rows(grads):
    owners, shards_n = lax.axis_size("dp"), lax.axis_size("tensor")
    stack = jnp.stack([g.astype(BF) for g in grads])
    count, rows, width = stack.shape
    stack = stack.reshape(count, shards_n, rows // shards_n, owners, width // owners)
    stack = stack.transpose(3, 1, 0, 2, 4).reshape(
        owners * shards_n, count, rows // shards_n, width // owners
    )
    out = lax.psum_scatter(stack, AXES, scatter_dimension=0, tiled=True)
    return out[0].astype(F32)


def sum_all(value):
    for axis in AXES:
        size = lax.axis_size(axis)
        bit = 1
        while bit < size:
            value = value + lax.ppermute(value, axis, [(i, i ^ bit) for i in range(size)])
            bit *= 2
    return value


def soap_block(grad_block, first, second, left, right, step_size, beta_one, beta_two):
    half_turn = jnp.einsum("kab,kac->kbc", left, grad_block, precision=PRECISE)
    rotated = jnp.einsum("kbc,kce->kbe", half_turn, right, precision=PRECISE)
    first_new = beta_one * first + (1.0 - beta_one) * rotated
    second_new = beta_two * second + (1.0 - beta_two) * rotated * rotated
    direction = first_new / (jnp.sqrt(second_new) + ADAM_EPS)
    back_half = jnp.einsum("kab,kbe->kae", left, direction, precision=PRECISE)
    turned = jnp.einsum("kae,kce->kac", back_half, right, precision=PRECISE)
    factor = jnp.sqrt(jnp.mean(direction * direction, axis=(1, 2))) * lax.rsqrt(
        jnp.mean(turned * turned, axis=(1, 2)) + SCALE_EPS
    )
    update = -step_size * factor[:, None, None] * turned
    return (first_new, second_new, update, factor)


def per_device(
    hidden_in,
    out_grad,
    attn_weight,
    mlp_weight,
    norm_gain,
    attn_first,
    attn_second,
    attn_left,
    attn_right,
    mlp_first,
    mlp_second,
    mlp_left,
    mlp_right,
    gain_first,
    gain_second,
    owner_rows,
    segment_ids,
    positions,
    valid,
    step,
    learn_rate,
    beta_first,
    beta_second,
):
    owners = lax.axis_size("dp")
    shards = lax.axis_size("tensor")
    rows = hidden_in.shape[0]
    slab = D // owners
    parts = SEQ_LEN // rows
    place = lax.axis_index("tensor")
    part = place % parts
    ahead = [(i, i - i % parts + (i + 1) % parts) for i in range(shards)]
    behind = [(j, i) for i, j in ahead]

    hidden_parts = [hidden_in]
    for _ in range(parts - 1):
        hidden_parts.append(lax.ppermute(hidden_parts[-1], "tensor", ahead))

    def of_sequence(values):
        here = lax.dynamic_index_in_dim(
            values.reshape(-1, parts, rows), place // parts, 0, keepdims=False
        )
        turned = jnp.concatenate([here[::-1], here[::-1]], axis=0)
        return lax.dynamic_slice_in_dim(turned, parts - 1 - part, parts, 0).reshape(SEQ_LEN)

    seg_all, pos_all, keep_all = of_sequence(segment_ids), of_sequence(positions), of_sequence(valid)

    attn_t = attn_weight.transpose(0, 2, 1)
    mlp_t = mlp_weight.transpose(0, 2, 1)
    qkv_t = gather_rows(attn_t[:3])
    out_t = gather_rows(attn_t[3:])[0]
    gate_up_t = gather_rows(mlp_t[:2])
    down_t = gather_rows(mlp_t[2:])[0]

    feature = (owner_rows[:, None] * slab + jnp.arange(slab, dtype=jnp.int32)[None, :]).reshape(D)
    to_place = (jnp.arange(D, dtype=jnp.int32)[:, None] == feature[None, :]).astype(BF)
    gain_rows = jnp.dot(norm_gain, to_place, preferred_element_type=F32)

    hidden_all = dot(jnp.concatenate(hidden_parts, axis=0), to_place)
    hidden_own = hidden_all[:rows]
    grad_own = dot(out_grad, to_place)
    grad_low = grad_own.astype(BF)

    first_all = (norm_stats(hidden_all)[0] * gain_rows[0]).astype(BF)
    first_own = first_all[:rows]
    half = HEAD_DIM // 2
    frequency = jnp.exp(jnp.arange(half, dtype=F32) * (-2.0 * math.log(ROPE_BASE) / HEAD_DIM))
    angles = pos_all.astype(F32)[:, None] * frequency[None, :]
    cosine, sine = jnp.cos(angles), jnp.sin(angles)
    cosine = jnp.tile(cosine, (1, 4))
    sine = jnp.tile(jnp.concatenate([-sine, sine], axis=1), (1, 2))
    attended, queries, key_rows, value_rows, weights, inverse_sums = attn_fwd(
        dot(first_own, qkv_t[0], NT),
        dot(first_all, qkv_t[1], NT),
        dot(first_all, qkv_t[2], NT),
        cosine,
        sine,
        seg_all[None, :rows],
        seg_all[:, None],
        keep_all[:, None],
    )
    attn_branch = dot(attended, out_t)
    resid = hidden_own + attn_branch
    second_norm = (norm_stats(resid)[0] * gain_rows[1]).astype(BF)
    gate = dot(second_norm, gate_up_t[0], NT)
    up = dot(second_norm, gate_up_t[1], NT)
    normal = 0.5 * (1.0 + lax.erf(gate * math.sqrt(0.5)))
    density = jnp.exp(-0.5 * gate * gate) * (1.0 / math.sqrt(2.0 * math.pi))
    gelu = gate * normal
    activated = (gelu * up).astype(BF)
    by_up = gelu.astype(BF)
    by_gate = (up * (normal + gate * density)).astype(BF)
    mlp_branch = dot(activated, down_t)
    result = resid + mlp_branch
    output = dot(result.astype(BF), to_place, NT).astype(BF)
    keep_own = lax.dynamic_slice_in_dim(valid, place * rows, rows, 0).astype(F32)[:, None]
    stat_terms = jnp.stack(
        [
            jnp.sum(keep_own),
            jnp.sum(keep_own * attn_branch * attn_branch),
            jnp.sum(keep_own * resid * resid),
            jnp.sum(keep_own * mlp_branch * mlp_branch),
            jnp.sum(keep_own * result * result),
        ]
    )

    hidden_grad = dot(grad_low, down_t, NT)
    gate_grad = (hidden_grad * by_gate).astype(BF)
    up_grad = (hidden_grad * by_up).astype(BF)
    mlp_grads = scatter_rows(
        [
            dot(gate_grad, second_norm, TN),
            dot(up_grad, second_norm, TN),
            dot(activated, grad_low, TN),
        ]
    )
    second_grad = dot(gate_grad, gate_up_t[0]) + dot(up_grad, gate_up_t[1])
    resid_part, gain_two = norm_back(resid, gain_rows[1], second_grad)
    resid_grad = grad_own + resid_part
    resid_low = resid_grad.astype(BF)
    mixed_grad = dot(resid_low, out_t, NT).astype(BF)
    out_wgrad = dot(attended, resid_low, TN)
    dq, dk, dv = attn_bwd(
        queries, key_rows, value_rows, attended, mixed_grad, weights, inverse_sums, cosine, sine
    )
    attn_grads = scatter_rows(
        [dot(dq, first_own, TN), dot(dk, first_all, TN), dot(dv, first_all, TN), out_wgrad]
    )
    late = dot(dk, qkv_t[1]) + dot(dv, qkv_t[2])
    others = dot(late[rows:].astype(BF), to_place, NT).astype(BF)
    passed = None
    for back in range(parts - 1, 0, -1):
        mine = others[(back - 1) * rows : back * rows]
        if passed is not None:
            mine = (mine.astype(F32) + passed.astype(F32)).astype(BF)
        passed = lax.ppermute(mine, "tensor", behind)
    first_grad = dot(dq, qkv_t[0]) + late[:rows]
    if passed is not None:
        first_grad = first_grad + dot(passed, to_place)
    input_part, gain_one = norm_back(hidden_own, gain_rows[0], first_grad)
    input_grad = dot((resid_grad + input_part).astype(BF), to_place, NT).astype(BF)

    gain_part = lax.dot_general(
        jnp.stack([gain_one, gain_two]),
        to_place.astype(F32),
        NT,
        precision=PRECISE,
        preferred_element_type=F32,
    )
    sums = sum_all(
        jnp.concatenate([gain_part, jnp.pad(stat_terms, (0, D - 5))[None]], axis=0)
    )
    gain_grad, stat_sums = sums[:2], sums[2, :5]

    attn_grad = attn_grads.transpose(0, 2, 1)
    mlp_grad = mlp_grads.transpose(0, 2, 1)
    step_count = step.astype(F32)
    step_size = (
        learn_rate
        * jnp.sqrt(1.0 - jnp.power(beta_second, step_count))
        / (1.0 - jnp.power(beta_first, step_count))
    )
    attn_first_new, attn_second_new, attn_update, attn_scale = soap_block(
        attn_grad, attn_first, attn_second, attn_left, attn_right, step_size, beta_first, beta_second
    )
    mlp_first_new, mlp_second_new, mlp_update, mlp_scale = soap_block(
        mlp_grad, mlp_first, mlp_second, mlp_left, mlp_right, step_size, beta_first, beta_second
    )
    gain_first_new = beta_first * gain_first + (1.0 - beta_first) * gain_grad
    gain_second_new = beta_second * gain_second + (1.0 - beta_second) * gain_grad * gain_grad
    gain_update = -step_size * gain_first_new / (jnp.sqrt(gain_second_new) + ADAM_EPS)
    root_means = jnp.sqrt(stat_sums[1:] / (stat_sums[0] * D))
    norm_scale = jnp.concatenate([attn_scale, mlp_scale], axis=0).reshape(7, 1, 1)
    return (
        output,
        input_grad,
        attn_grad,
        mlp_grad,
        gain_grad,
        attn_first_new,
        attn_second_new,
        mlp_first_new,
        mlp_second_new,
        gain_first_new,
        gain_second_new,
        attn_update,
        mlp_update,
        gain_update,
        norm_scale,
        root_means,
    )


def solution(mesh):
    tokens, matrices, whole, group = P(AXES, None), P(None, "dp", "tensor"), P(), P("dp")
    return jax.shard_map(
        per_device,
        mesh=mesh,
        in_specs=(tokens, tokens, matrices, matrices, whole)
        + (matrices,) * 8
        + (whole,) * 3
        + (group,) * 3
        + (whole,) * 4,
        out_specs=(tokens, tokens, matrices, matrices, whole)
        + (matrices,) * 4
        + (whole,) * 2
        + (matrices,) * 2
        + (whole, matrices, whole),
        check_vma=False,
    )
```

time: 1550 us -> 875 us (0.56)
  waiting for transfers between devices: 833 us -> 522 us
  matrix products: 332 us -> 150 us
  local copies, waits for them, and re-layouts: 192 us -> 105 us
  other arithmetic: 102 us -> 15.4 us
  Pallas kernels: 0 us -> 45.1 us
  blocking collectives: 41 us -> 0 us
    reduce_scatter x6 -> x2, waiting for transfers between devices: 544 us -> 263 us  [scatter_rows(): out = lax.psum_scatter(stack, AXES, scatter_dimension=0, tiled=True)]
    dot_general x40 -> x29, matrix products: 304 us -> 123 us  [the longest x27 120 us: dot(): return lax.dot_general(a, b, dims, preferred_element_type=F32)]
    all_gather x6 -> x4, waiting for transfers between devices: 287 us -> 190 us  [gather_rows(): got = lax.all_gather(shards, AXES, axis=0, tiled=False)]
    ppermute x0 -> x7, waiting for transfers between devices: none -> 68.9 us  [the longest x1 45.4 us: per_device(): passed = lax.ppermute(mine, 'tensor', behind)]
    dynamic_update_slice x12 -> x0, local copies, waits for them, and re-layouts: 51.9 us -> none  [per_device(): lax.map(sequence_forward, (queries, key_rows, value_rows, seg_seq, keep_s...]
    pallas_call x0 -> x2, Pallas kernels: none -> 45.1 us  [the longest x1 22.7 us: attn_fwd(): pl.pallas_call(functools.partial(fwd_kernel, chunk), grid=(pairs,), in_sp...]
    psum x1 -> x0, blocking collectives: 41 us -> none  [per_device(): gain_grad = lax.psum(gain_part, ('dp', 'tensor'))]
    reshape x5 -> x7, local copies, waits for them, and re-layouts: 11.1 us -> 42 us  [the longest x4 42 us: gather_rows(): got.reshape(owners, shards_n, count, rows, slab).transpose(2, 1, 3, 0, 4)]
  transfers between devices with their start and end apart: 12 -> 13, of which waited for: 11 -> 11; matrix products, arithmetic and copies ran while one was open for 34% -> 15% of each run, Pallas kernels for 0% -> 3%
where the time goes in v1:
time: 875 us; the launch traced here: 864 us
  waiting for transfers between devices  522 us (60%)
  matrix products  150 us (17%)
  local copies, waits for them, and re-layouts  105 us (12%)
  Pallas kernels  45.1 us (5%)
  between operations  18.8 us (2%)
  other arithmetic  15.4 us (2%)
    reduce_scatter x2, waiting for transfers between devices, scatter_rows(): out = lax.psum_scatter(stack, AXES, scatter_dimension=0, tiled=True)  263 us
    all_gather x4, waiting for transfers between devices, gather_rows(): got = lax.all_gather(shards, AXES, axis=0, tiled=False)  190 us
    dot_general x27, matrix products, dot(): return lax.dot_general(a, b, dims, preferred_element_type=F32)  120 us
    ppermute x1, waiting for transfers between devices, per_device(): passed = lax.ppermute(mine, 'tensor', behind)  45.4 us
    reshape x4, local copies, waits for them, and re-layouts, gather_rows(): got.reshape(owners, shards_n, count, rows, slab).transpose(2, 1, 3, 0, 4)  42 us
    pallas_call x1, Pallas kernels, attn_fwd(): pl.pallas_call(functools.partial(fwd_kernel, chunk), grid=(pairs,), in_sp...  22.7 us
    pallas_call x1, Pallas kernels, attn_bwd(): pl.pallas_call(functools.partial(bwd_kernel, chunk), grid=(pairs,), in_sp...  22.4 us
    transpose x2, local copies, waits for them, and re-layouts, scatter_rows(): stack.transpose(3, 1, 0, 2, 4)  22.1 us
  transfers between devices with their start and end apart: 13, of which 11 were waited for; matrix products, arithmetic and copies ran while one was open for 15% of the time, Pallas kernels for 3%

profile of v1, /device:TPU:0, one launch (start us, length us, event | category | flops | bytes accessed | tf_op | source)
XLA Modules:
  0.0 863.9 jit_solution(16848899783192644799)
XLA Ops:
  13.5 3.1 collective-permute-start
  24.1 2.6 fusion.39
  26.7 14.6 %collective-permute-done = bf16[512,1024]{1,0:T(8,128)(2,1)} collective-permute-done((bf16[512,1024]{1,0:T(8,128)(2,1)S(1)}, bf16[512,1024]{1,0:T(8,128)(2,1)}, u32[]{:S(2)}, u32[]{:S(2)}) %collective-permute-start) | collective-permute-done | bytes 1048608 | tf_op jit(solution)/shard_map/ppermute | solution.py:240
  41.3 3.6 fusion.130
  47.4 23.3 %all-gather.11.cloned.1.call-done = bf16[32,256,128]{2,1,0:T(8,128)(2,1)} async-done(((bf16[1,256,128]{2,1,0:T(8,128)(2,1)}), bf16[32,256,128]{2,1,0:T(8,128)(2,1)}) %all-gather.11.cloned.1.call-update) | async-done | bytes 2097168 | tf_op jit(solution)/shard_map/all_gather | solution.py:160
  70.7 4.3 copy.81
  75.0 63.9 %all-gather.15.cloned.1.call-done = bf16[32,656,128]{2,1,0:T(8,128)(2,1)} async-done(((bf16[1,656,128]{2,1,0:T(8,128)(2,1)}), bf16[32,656,128]{2,1,0:T(8,128)(2,1)}) %all-gather.15.cloned.1.call-update) | async-done | bytes 5373968 | tf_op jit(solution)/shard_map/all_gather | solution.py:160
  138.9 8.4 copy.84
  147.3 62.9 %all-gather.9.cloned.1.call-done = bf16[96,256,128]{2,1,0:T(8,128)(2,1)} async-done(((bf16[3,256,128]{2,1,0:T(8,128)(2,1)}), bf16[96,256,128]{2,1,0:T(8,128)(2,1)}) %all-gather.9.cloned.1.call-update) | async-done | bytes 6291472 | tf_op jit(solution)/shard_map/all_gather | solution.py:160
  210.1 8.1 copy.202
  218.7 3.1 fusion.55.qraw
  221.8 4.4 fusion.47.vraw
  226.2 4.5 fusion.51.kraw
  230.7 22.7 %attn_fwd.1 = (bf16[512,1024]{1,0:T(8,128)(2,1)}, bf16[512,1024]{1,0:T(8,128)(2,1)}, bf16[1024,1024]{1,0:T(8,128)(2,1)}, bf16[1024,1024]{1,0:T(8,128)(2,1)}, bf1...) custom-call(f32[512,1024]{1,0:T(8,128)} %fusion.55.qraw, f32[1024,1024]{1,0:T(8,128)} %fusion.51.kraw, ...), custom_call_target="tpu_custom_call" | custom-call | flops 2147483648 | bytes 29360128 | tf_op jit(solution)/shard_map/attn_fwd/pallas_call | solution.py:77
  253.4 5.9 fusion.126
  259.9 39.6 %all-gather.13.cloned.1.call-done = bf16[64,656,128]{2,1,0:T(8,128)(2,1)} async-done(((bf16[2,656,128]{2,1,0:T(8,128)(2,1)}), bf16[64,656,128]{2,1,0:T(8,128)(2,1)}) %all-gather.13.cloned.1.call-update) | async-done | bytes 10747920 | tf_op jit(solution)/shard_map/all_gather | solution.py:160
  299.5 21.2 %copy.201 = bf16[8,4,2,656,128]{4,0,3,1,2:T(8,128)(2,1)} copy(bf16[8,4,2,656,128]{4,3,2,1,0:T(8,128)(2,1)} %bitcast.230) | data formatting | bytes 21495808 | tf_op jit(solution)/shard_map/reshape | solution.py:162
  320.7 8.9 %fusion.127 = (bf16[1,4,656,8,128]{4,3,2,1,0:T(8,128)(2,1)}, bf16[1,4,656,8,128]{4,3,2,1,0:T(8,128)(2,1)}) fusion(bf16[2,4,656,8,128]{4,3,2,1,0:T(8,128)(2,1)} %bitcast.222), kind=kLoop, calls=%fused_computation.206 | loop fusion | bytes 21495808 | tf_op jit(solution)/shard_map/slice | solution.py:288
  329.6 7.4 fusion.12
  337.1 4.6 fusion.16
  341.7 10.9 %multiply_convert_fusion.1 = (bf16[512,2624]{0,1:T(8,128)(2,1)}, bf16[512,2624]{0,1:T(8,128)(2,1)}, bf16[512,2624]{0,1:T(8,128)(2,1)}) fusion(f32[512,2624]{0,1:T(8,128)} %fusion.12, f32[512,2624]{0,1:T(8,128)} %fusion.16, bf16[328,8,8,128]{3,2,1,0:T(8,128)(2,1)S(1)} %bitcast.241, f32[1024,512]{1,0:T(8,128)S(1)} %copy-done.11), kind=kOutput, calls=%fused_computation.27 | convolution fusion | flops 2778333184 | bytes 26279936 | tf_op jit(solution)/shard_map/dot_general | solution.py:28
  352.7 6.4 fusion.10
  359.1 3.2 fusion.8
  362.3 8.6 multiply_reduce_fusion.1
  374.8 2.6 convert_bitcast_fusion
  377.5 22.4 %attn_bwd.1 = (bf16[512,1024]{1,0:T(8,128)(2,1)}, bf16[1024,1024]{1,0:T(8,128)(2,1)}, bf16[1024,1024]{1,0:T(8,128)(2,1)}) custom-call(bf16[512,1024]{1,0:T(8,128)(2,1)} %get-tuple-element.26.q_ref, bf16[1024,1024]{1,0:T(8,128)(2,1)} %get-tuple-element.27.k_ref, bf16[1024,1024]{1,0:T(8,128)(2,1)} %get-tuple-element.28.v_ref, ...), custom_call_target="tpu_custom_call" | custom-call | flops 4294967296 | bytes 29360128 | tf_op jit(solution)/shard_map/attn_bwd/pallas_call | solution.py:130
  399.9 2.8 convert_bitcast_fusion.3
  413.6 3.9 maximum_bitcast_fusion.1
  417.4 13.7 %copy.92 = bf16[8,4,4,256,128]{3,4,2,1,0:T(8,128)(2,1)} copy(bf16[8,4,4,256,128]{4,0,3,1,2:T(8,128)(2,1)} %maximum_bitcast_fusion.1) | data formatting | bytes 16777216 | tf_op jit(solution)/shard_map/transpose | solution.py:171
  432.4 5.1 fusion.32
  439.2 3.3 fusion.33
  444.2 6.6 fusion.34
  450.7 3.9 copy.132
  456.6 8.5 copy.93
  465.1 4.9 fusion.45
  476.3 3.3 stack.71
  479.6 3.4 fusion.53
  483.0 45.4 %collective-permute-done.1 = bf16[512,1024]{1,0:T(8,128)(2,1)} collective-permute-done((bf16[512,1024]{1,0:T(8,128)(2,1)}, bf16[512,1024]{1,0:T(8,128)(2,1)}, u32[]{:S(2)}, u32[]{:S(2)}) %collective-permute-start.1) | collective-permute-done | bytes 1048608 | tf_op jit(solution)/shard_map/ppermute | solution.py:339
  528.4 5.2 multiply_reduce_fusion.2
  538.4 2.8 collective-permute-start.3
  541.2 4.4 fusion.86
  546.4 3.1 collective-permute-done.4
  549.5 4.8 collective-permute-done.5
  554.4 4.7 fusion.88
  562.5 76.3 %reduce-scatter.3.cloned.1.call-done = bf16[1,4,256,128]{2,3,1,0:T(8,128)(2,1)} async-done(((bf16[32,4,256,128]{2,3,1,0:T(8,128)(2,1)}), bf16[1,4,256,128]{2,3,1,0:T(8,128)(2,1)}) %reduce-scatter.3.cloned.1.call-update) | async-done | bytes 262160 | tf_op jit(solution)/shard_map/reduce_scatter | solution.py:174
  645.2 186.7 %reduce-scatter.5.cloned.1.call-done = bf16[1,3,656,128]{3,2,1,0:T(8,128)(2,1)} async-done(((bf16[32,3,656,128]{3,2,1,0:T(8,128)(2,1)}), bf16[1,3,656,128]{3,2,1,0:T(8,128)(2,1)}) %reduce-scatter.5.cloned.1.call-update) | async-done | bytes 503824 | tf_op jit(solution)/shard_map/reduce_scatter | solution.py:174
  833.7 13.7 %multiply_reduce_fusion.10 = (f32[3]{0:T(128)S(1)}, f32[3,128,656]{1,2,0:T(8,128)S(1)}, f32[3,128,656]{1,2,0:T(8,128)S(1)}) fusion(f32[]{:T(128)S(6)} %sub.92, f32[3,128,656]{1,2,0:T(8,128)S(1)} %copy-done.25, f32[]{:T(128)S(6)} %copy.206, f32[]{:T(128)S(6)} %sub.91, f32[3,128,656]{1,2,0:T(8,128)S(1)} %copy-done.26, f32[]{:T(128)S(6)} %copy.205, ...), kind=kOutput, calls=%fused_computation.129 | convolution fusion | flops 1985759232 | bytes 10202140 | tf_op jit(solution)/shard_map/kbc,kce->kbe/dot_general | solution.py:190
  848.9 5.3 multiply_reduce_fusion.9
  (237 shorter events, 62.1 us)
Async XLA Ops:
  7.2 16.9 %copy-start = (bf16[512,1024]{1,0:T(8,128)(2,1)S(1)}, bf16[512,1024]{1,0:T(8,128)(2,1)}, u32[]{:S(2)}) copy-start(bf16[512,1024]{1,0:T(8,128)(2,1)} %param.24) | copy-start | bytes 3145732
  7.2 6.3 copy-start.50
  7.2 9.4 %copy-start.41 = (s32[2048]{0:T(1024)S(1)}, s32[2048]{0:T(1024)}, u32[]{:S(2)}) copy-start(s32[2048]{0:T(1024)} %param.40) | copy-start | bytes 24580
  7.2 63.5 %all-gather.11.cloned.1.call-start = ((), (), s32[]{:S(2)}) async-start(), calls=%async_computation.5 | async-start | bytes 2162688 | tf_op jit(solution)/shard_map/all_gather | solution.py:160
  9.2 129.7 %all-gather.15.cloned.1.call-start = ((), (), s32[]{:S(2)}) async-start(), calls=%async_computation.7 | async-start | bytes 5541888 | tf_op jit(solution)/shard_map/all_gather | solution.py:160
  10.9 199.3 %all-gather.9.cloned.1.call-start = ((), (), s32[]{:S(2)}) async-start(), calls=%async_computation.4 | async-start | bytes 6488064 | tf_op jit(solution)/shard_map/all_gather | solution.py:160
  11.6 287.9 %all-gather.13.cloned.1.call-start = ((), (), s32[]{:S(2)}) async-start(), calls=%async_computation.6 | async-start | bytes 11083776 | tf_op jit(solution)/shard_map/all_gather | solution.py:160
  13.4 625.3 %reduce-scatter.3.cloned.1.call-start = ((), (), s32[]{:S(2)}) async-start(), calls=%async_computation.2 | async-start | bytes 8650752 | tf_op jit(solution)/shard_map/reduce_scatter | solution.py:174
  13.5 27.8 %collective-permute-start = (bf16[512,1024]{1,0:T(8,128)(2,1)S(1)}, bf16[512,1024]{1,0:T(8,128)(2,1)}, u32[]{:S(2)}, u32[]{:S(2)}) collective-permute-start(bf16[512,1024]{1,0:T(8,128)(2,1)S(1)} %copy-done.50), channel_id=1, source_target_pairs={{0,1},{1,0},{2,3},{3,2},{4,5},{5,4},{6,7},{7,6},{8,9},{9,8},{10,11... | collective-permute-start | bytes 3145736 | tf_op jit(solution)/shard_map/ppermute | solution.py:240
  17.5 5.8 copy-start.51
  23.3 18.0 %copy-start.45 = (s32[1024]{0:T(1024)}, s32[1024]{0:T(1024)S(1)}, u32[]{:S(2)}) copy-start(s32[1024]{0:T(1024)S(1)} %add_bitcast_fusion) | copy-start | bytes 12292
  24.1 21.6 %copy-start.35 = (f32[1,1024]{1,0:T(1,128)}, f32[1,1024]{1,0:T(1,128)S(1)}, u32[]{:S(2)}) copy-start(f32[1,1024]{1,0:T(1,128)S(1)} %get-tuple-element.75) | copy-start | bytes 12292
  45.2 208.2 %copy-start.38 = (f32[512]{0:T(512)}, f32[512]{0:T(512)S(1)}, u32[]{:S(2)}) copy-start(f32[512]{0:T(512)S(1)} %broadcast_multiply_fusion.5) | copy-start | bytes 6148
  47.4 178.8 %copy-start.14 = (bf16[1024,1024]{0,1:T(8,128)(2,1)}, bf16[1024,1024]{0,1:T(8,128)(2,1)S(1)}, u32[]{:S(2)}) copy-start(bf16[1024,1024]{0,1:T(8,128)(2,1)S(1)} %multiply_convert_fusion.3) | copy-start | bytes 6291460
  218.7 7.5 copy-start.18
  259.9 77.2 %copy-start.22 = (bf16[512,1024]{0,1:T(8,128)(2,1)}, bf16[512,1024]{0,1:T(8,128)(2,1)S(1)}, u32[]{:S(2)}) copy-start(bf16[512,1024]{0,1:T(8,128)(2,1)S(1)} %multiply_convert_fusion.4) | copy-start | bytes 3145732
  329.6 7.4 copy-start.6
  329.6 12.1 %slice-start.2 = ((s8[5373952]{0:T(1024)(128)(4,1)}), s8[4194304]{0:T(1024)(128)(4,1)S(1)}, s32[]{:S(2)}) async-start(s8[5373952]{0:T(1024)(128)(4,1)} %bitcast.239), calls=%async_computation.10 | async-start | bytes 8388608
  337.0 15.6 %slice-start.4 = ((s8[5373952]{0:T(1024)(128)(4,1)}), s8[4194304]{0:T(1024)(128)(4,1)S(1)}, s32[]{:S(2)}) async-start(s8[5373952]{0:T(1024)(128)(4,1)} %bitcast.246), calls=%async_computation.12 | async-start | bytes 8388608
  341.7 11.0 %slice-start.5 = ((s8[5373952]{0:T(1024)(128)(4,1)}), s8[1179648]{0:T(1024)(128)(4,1)S(1)}, s32[]{:S(2)}) async-start(s8[5373952]{0:T(1024)(128)(4,1)} %bitcast.246), calls=%async_computation.13 | async-start | bytes 2359296
  352.7 6.4 copy-start.55
  362.3 8.6 copy-start.54
  431.2 400.8 %reduce-scatter.5.cloned.1.call-start = ((), (), s32[]{:S(2)}) async-start(), calls=%async_computation.3 | async-start | bytes 16625664 | tf_op jit(solution)/shard_map/reduce_scatter | solution.py:174
  474.9 53.4 %collective-permute-start.1 = (bf16[512,1024]{1,0:T(8,128)(2,1)}, bf16[512,1024]{1,0:T(8,128)(2,1)}, u32[]{:S(2)}, u32[]{:S(2)}) collective-permute-start(bf16[512,1024]{1,0:T(8,128)(2,1)} %fusion.87), channel_id=1, source_target_pairs={{1,0},{0,1},{3,2},{2,3},{5,4},{4,5},{7,6},{6,7},{9,8},{8,9},{11,10... | collective-permute-start | bytes 3145736 | tf_op jit(solution)/shard_map/ppermute | solution.py:339
  479.6 48.8 %copy-start.3 = (f32[1024,1024]{0,1:T(8,128)S(1)}, f32[1024,1024]{0,1:T(8,128)}, u32[]{:S(2)}) copy-start(f32[1024,1024]{0,1:T(8,128)} %copy-done.2) | copy-start | bytes 12582916
  479.6 48.8 %copy-start.36 = (f32[1,1024]{1,0:T(1,128)S(1)}, f32[1,1024]{1,0:T(1,128)}, u32[]{:S(2)}) copy-start(f32[1,1024]{1,0:T(1,128)} %copy-done.35) | copy-start | bytes 12292
  479.6 48.8 %copy-start.39 = (f32[512]{0:T(512)S(1)}, f32[512]{0:T(512)}, u32[]{:S(2)}) copy-start(f32[512]{0:T(512)} %copy-done.38) | copy-start | bytes 6148
  535.5 2.9 collective-permute-start.2
  538.4 16.0 %copy-start.4 = (f32[1024,1024]{0,1:T(8,128)S(1)}, f32[1024,1024]{0,1:T(8,128)}, u32[]{:S(2)}) copy-start(f32[1024,1024]{0,1:T(8,128)} %copy-done.2) | copy-start | bytes 12582916
  538.4 16.0 %copy-start.10 = (f32[512,1024]{0,1:T(8,128)S(1)}, f32[512,1024]{0,1:T(8,128)}, u32[]{:S(2)}) copy-start(f32[512,1024]{0,1:T(8,128)} %copy-done.9) | copy-start | bytes 6291460
  538.4 7.2 collective-permute-start.3
  545.6 3.9 collective-permute-start.4
  549.5 4.8 collective-permute-start.5
  554.3 5.7 collective-permute-start.6
  554.4 7.5 copy-start.43
  554.4 7.5 copy-start.44
  554.4 84.4 %copy-start.33 = (f32[4,128,128]{2,1,0:T(8,128)S(1)}, f32[4,128,128]{2,1,0:T(8,128)}, u32[]{:S(2)}) copy-start(f32[4,128,128]{2,1,0:T(8,128)} %param.30) | copy-start | bytes 786436
  554.4 85.8 %copy-start.8 = (f32[4,256,256]{2,1,0:T(8,128)S(1)}, f32[4,256,256]{2,1,0:T(8,128)}, u32[]{:S(2)}) copy-start(f32[4,256,256]{2,1,0:T(8,128)} %param.31) | copy-start | bytes 3145732
  554.4 85.8 %copy-start.29 = (f32[4,128,256]{2,1,0:T(8,128)S(1)}, f32[4,128,256]{2,1,0:T(8,128)}, u32[]{:S(2)}) copy-start(f32[4,128,256]{2,1,0:T(8,128)} %param.29) | copy-start | bytes 1572868
  554.4 85.8 %copy-start.30 = (f32[4,128,256]{2,1,0:T(8,128)S(1)}, f32[4,128,256]{2,1,0:T(8,128)}, u32[]{:S(2)}) copy-start(f32[4,128,256]{2,1,0:T(8,128)} %param.28) | copy-start | bytes 1572868
  642.2 189.8 %copy-start.34 = (f32[3,128,128]{2,1,0:T(8,128)S(1)}, f32[3,128,128]{2,1,0:T(8,128)}, u32[]{:S(2)}) copy-start(f32[3,128,128]{2,1,0:T(8,128)} %param.34) | copy-start | bytes 589828
  643.4 190.3 %copy-start.25 = (f32[3,128,656]{1,2,0:T(8,128)S(1)}, f32[3,128,656]{1,2,0:T(8,128)}, u32[]{:S(2)}) copy-start(f32[3,128,656]{1,2,0:T(8,128)} %param.33) | copy-start | bytes 3022852
  643.4 190.3 %copy-start.26 = (f32[3,128,656]{1,2,0:T(8,128)S(1)}, f32[3,128,656]{1,2,0:T(8,128)}, u32[]{:S(2)}) copy-start(f32[3,128,656]{1,2,0:T(8,128)} %param.32) | copy-start | bytes 3022852
  832.0 16.9 %slice-start = ((s8[6045696]{0:T(1024)(128)(4,1)}), s8[4194304]{0:T(1024)(128)(4,1)S(1)}, s32[]{:S(2)}) async-start(s8[6045696]{0:T(1024)(128)(4,1)} %bitcast.225), calls=%async_computation.8 | async-start | bytes 8388608
  833.7 15.1 %slice-start.1 = ((s8[6045696]{0:T(1024)(128)(4,1)}), s8[1851392]{0:T(1024)(128)(4,1)S(1)}, s32[]{:S(2)}) async-start(s8[6045696]{0:T(1024)(128)(4,1)} %bitcast.225), calls=%async_computation.9 | async-start | bytes 3702784
  847.4 6.7 copy-start.27
  847.5 6.7 copy-start.28
  848.8 8.0 copy-start.1
  (28 other events, 76.1 us)
Sparse Core Ops, SparseCore 0:
  11.5 59.1 all-gather.10
  74.1 64.7 all-gather.14
  142.4 67.7 all-gather.8
  213.4 86.0 all-gather.12
  431.3 207.4 reduce-scatter.2
  645.0 186.9 reduce-scatter.4
